TPU v7x, 512 devices: a whole 4x4x16 slice. The times are simulated.
512 devices in a mesh: ctx: 64 (over x, z), tp: 8 (over y, core).
Axes of the slice: x: 4, y: 4, z: 16, core: 2. Of those that a mesh axis runs over, the one named last changes fastest.
Arguments:
- projected: bfloat16 [16384, 3, 4096], P('ctx', None, 'tp'), may hold values from -6 to 6
- short_filter: float32 [3, 3, 4096], P(None, None, 'tp'), may hold values from -3 to 3
- residues: float32 [4096, 16], P('tp'), may hold values from -3 to 3
- rates: float32 [4096, 16], P('tp'), may hold values from 3.0517577e-07 to 0.05
- skip_gain: float32 [4096], P('tp'), may hold values from -3 to 3
- out_weight: bfloat16 [4096, 4096], P('tp', 'ctx'), may hold values from -0.09375 to 0.09375
Outputs:
- mixed: bfloat16 [16384, 4096], P('ctx', 'tp')
All inputs are finite; a program needn't handle non-finite values.
Results may differ from a plain program's by a relative error of at most 0.019.
Values may be sent and summed in bfloat16 or wider, within the bound.
A program may use at most 64 MiB of HBM per device.

v0:
```python
import math

import jax
import jax.numpy as jnp
from jax import lax
from jax.sharding import PartitionSpec as P

HIGHEST_PREC = lax.Precision.HIGHEST


def from_behind(value, axis, steps):
    count = lax.axis_size(axis)
    initial, last = (max(0, -steps), min(count, count - steps))
    return lax.ppermute(value, axis, [(source, source + steps) for source in range(initial, last)])


def for_sending(shard):
    return jax.tree.map(lambda a: a.astype(jnp.bfloat16) if a.dtype == jnp.float32 else a, shard)


def angle_table(first, second, period):
    return 2.0 * math.pi / period * (first * second % period).astype(jnp.float32)


def short_mix(projected, short_filter):
    earlier = from_behind(projected[-2:], "ctx", 1)
    padded = jnp.concatenate([earlier, projected], axis=0).astype(jnp.float32)
    mixture = (
        short_filter[0][None] * padded[2:]
        + short_filter[1][None] * padded[1:-1]
        + short_filter[2][None] * padded[:-2]
    )
    return mixture


def spectral_conv(gated_rows, mode_coef, rates):
    row_count, chan_count = gated_rows.shape
    ctx_count = lax.axis_size("ctx")
    ctx_place = lax.axis_index("ctx")
    full_span = 2 * row_count * ctx_count
    group_rows = row_count // ctx_count
    source_idx = jnp.arange(ctx_count, dtype=jnp.int32)
    freq_col = jnp.arange(2 * ctx_count, dtype=jnp.int32)
    local_rows = jnp.arange(group_rows, dtype=jnp.int32)
    columns = lax.all_to_all(
        gated_rows[None].astype(jnp.bfloat16), "ctx", split_axis=1, concat_axis=0, tiled=True
    ).astype(jnp.float32)
    phase_tab = angle_table(freq_col[:, None], source_idx[None, :], 2 * ctx_count)
    spec_re = jnp.einsum("kp,pjc->kjc", jnp.cos(phase_tab), columns, precision=HIGHEST_PREC)
    spec_im = -jnp.einsum("kp,pjc->kjc", jnp.sin(phase_tab), columns, precision=HIGHEST_PREC)
    sample_idx = ctx_place * group_rows + local_rows
    twist_tab = angle_table(freq_col[:, None], sample_idx[None, :], full_span)[:, :, None]
    cos_tab = jnp.cos(twist_tab)
    sin_tab = jnp.sin(twist_tab)
    columns_spec = jnp.stack(
        [spec_re * cos_tab + spec_im * sin_tab, spec_im * cos_tab - spec_re * sin_tab]
    )
    partial_spec = lax.all_to_all(
        for_sending(columns_spec), "ctx", split_axis=1, concat_axis=2, tiled=True
    ).astype(columns_spec.dtype)
    part_re = partial_spec[0]
    part_im = partial_spec[1]
    sample_all = jnp.arange(row_count, dtype=jnp.int32)
    local_angle = angle_table(sample_all[:, None], sample_all[None, :], row_count)
    cos_local = jnp.cos(local_angle)
    sin_local = jnp.sin(local_angle)
    spec_re = jnp.einsum("kj,ejc->ekc", cos_local, part_re, precision=HIGHEST_PREC) + jnp.einsum(
        "kj,ejc->ekc", sin_local, part_im, precision=HIGHEST_PREC
    )
    spec_im = jnp.einsum("kj,ejc->ekc", cos_local, part_im, precision=HIGHEST_PREC) - jnp.einsum(
        "kj,ejc->ekc", sin_local, part_re, precision=HIGHEST_PREC
    )
    parity_idx = jnp.arange(2, dtype=jnp.int32)
    first_freq = 2 * ctx_place + parity_idx
    freq_all = first_freq[:, None] + 2 * ctx_count * sample_all[None, :]
    angle_k = angle_table(freq_all, 1, full_span)[:, :, None]
    half_sin = jnp.sin(0.5 * angle_k)
    full_sin = jnp.sin(angle_k)
    parity_odd = (parity_idx == 1)[:, None, None]
    seq_length = row_count * ctx_count

    def add_mode(mode, filt_pair):
        rate_one = rates[:, mode][None, None, :]
        decay_one = jnp.exp(-rate_one)
        den_re = -jnp.expm1(-rate_one) + decay_one * 2.0 * half_sin * half_sin
        den_im = decay_one * full_sin
        numerator = jnp.where(
            parity_odd, 1.0 + jnp.exp(-rate_one * seq_length), -jnp.expm1(-rate_one * seq_length)
        )
        magnitude = den_re * den_re + den_im * den_im
        scale_one = mode_coef[:, mode][None, None, :] * numerator / magnitude
        return (filt_pair[0] + scale_one * den_re, filt_pair[1] - scale_one * den_im)

    filt_zero = jnp.zeros(spec_re.shape, jnp.float32)
    filt_re, filt_im = lax.fori_loop(0, rates.shape[1], add_mode, (filt_zero, filt_zero))
    prod_re = spec_re * filt_re - spec_im * filt_im
    prod_im = spec_re * filt_im + spec_im * filt_re
    back_re = jnp.einsum("kj,ekc->ejc", cos_local, prod_re, precision=HIGHEST_PREC) - jnp.einsum(
        "kj,ekc->ejc", sin_local, prod_im, precision=HIGHEST_PREC
    )
    back_im = jnp.einsum("kj,ekc->ejc", cos_local, prod_im, precision=HIGHEST_PREC) + jnp.einsum(
        "kj,ekc->ejc", sin_local, prod_re, precision=HIGHEST_PREC
    )
    turn_angle = angle_table(first_freq[:, None], sample_all[None, :], full_span)[:, :, None]
    turn_cos = jnp.cos(turn_angle)
    turn_sin = jnp.sin(turn_angle)
    turned = jnp.stack(
        [back_re * turn_cos - back_im * turn_sin, back_re * turn_sin + back_im * turn_cos]
    )
    gathered_spec = lax.all_to_all(
        for_sending(turned), "ctx", split_axis=2, concat_axis=1, tiled=True
    ).astype(turned.dtype)
    phase_tab = angle_table(source_idx[:, None], freq_col[None, :], 2 * ctx_count)
    summed_re = jnp.einsum(
        "pk,kjc->pjc", jnp.cos(phase_tab), gathered_spec[0], precision=HIGHEST_PREC
    )
    summed_im = jnp.einsum(
        "pk,kjc->pjc", jnp.sin(phase_tab), gathered_spec[1], precision=HIGHEST_PREC
    )
    signal_cols = (summed_re - summed_im) / full_span
    signal_rows = lax.all_to_all(
        for_sending(signal_cols), "ctx", split_axis=0, concat_axis=1, tiled=True
    ).astype(signal_cols.dtype)
    return signal_rows[0]


def per_device(projected, short_filter, residues, rates, skip_gain, out_weight):
    streams = short_mix(projected, short_filter)
    query_rows = streams[:, 0]
    gated_rows = streams[:, 1] * streams[:, 2]
    mode_coef = residues * jnp.sqrt(-jnp.expm1(-2.0 * rates))
    long_out = spectral_conv(gated_rows, mode_coef, rates)
    long_out = long_out + skip_gain[None, :] * gated_rows
    hidden = (query_rows * long_out).astype(jnp.bfloat16)
    partial_all = jnp.dot(
        hidden,
        lax.all_gather(out_weight, "ctx", axis=1, tiled=True),
        preferred_element_type=jnp.float32,
    )
    return lax.psum_scatter(partial_all.astype(jnp.bfloat16), "tp", scatter_dimension=1, tiled=True)


def solution(mesh):
    return jax.shard_map(
        per_device,
        mesh=mesh,
        in_specs=(
            P("ctx", None, "tp"),
            P(None, None, "tp"),
            P("tp", None),
            P("tp", None),
            P("tp"),
            P("tp", "ctx"),
        ),
        out_specs=P("ctx", "tp"),
        check_vma=False,
    )
```

profile of v0, /device:TPU:1, one launch (start us, length us, event | category | flops | bytes accessed | tf_op | source)
XLA Modules:
  0.0 295.2 jit_solution(16506021845243514412)
XLA Ops:
  6.5 0.7 slice.47
  7.3 4.4 %collective-permute-start = (bf16[2,3,512]{2,0,1:T(2,128)(2,1)S(1)}, bf16[2,3,512]{2,0,1:T(2,128)(2,1)S(1)}, u32[]{:S(2)}, u32[]{:S(2)}) collective-permute-start(bf16[2,3,512]{2,0,1:T(2,128)(2,1)S(1)} %slice.47), channel_id=1, source_target_pairs={{0,8},{8,16},{16,24},{24,32},{32,40},{40,48},{48,56},{56,64},{64,7... | collective-permute-start | bytes 18440 | tf_op jit(solution)/shard_map/ppermute | solution.py:14
  11.7 0.7 slice_bitcast_fusion.3
  12.4 1.4 maximum_convert_fusion
  14.3 1.1 copy-done
  16.4 2.2 reduce.2
  18.6 0.9 reshape.444
  19.5 19.6 %all-to-all-start = ((bf16[64,2,1024]{2,1,0:T(2,128)(2,1)}), bf16[64,2,1024]{2,1,0:T(2,128)(2,1)S(1)}, u32[]{:S(2)}, u32[]{:S(2)}) async-start(bf16[64,2,1024]{2,1,0:T(2,128)(2,1)} %reshape.444), calls=%async_computation | async-start | bytes 524288 | tf_op jit(solution)/shard_map/all_to_all | solution.py:45
  40.1 17.0 %all-to-all-done = bf16[64,2,1024]{2,1,0:T(2,128)(2,1)S(1)} async-done(((bf16[64,2,1024]{2,1,0:T(2,128)(2,1)}), bf16[64,2,1024]{2,1,0:T(2,128)(2,1)S(1)}, u32[]{:S(2)}, u32[]{:S(2)}) %all-to-all-start) | async-done | bytes 262176 | tf_op jit(solution)/shard_map/all_to_all | solution.py:45
  57.3 1.5 bitcast_reduce_fusion
  58.9 0.8 convolution_negate_fusion
  59.6 0.9 fusion.18
  60.7 1.8 copy.33
  62.5 8.0 %all-to-all-start.1 = ((bf16[2,128,4,512]{3,2,0,1:T(4,128)(2,1)}), bf16[2,128,4,512]{3,2,0,1:T(4,128)(2,1)S(1)}, u32[]{:S(2)}, u32[]{:S(2)}) async-start(bf16[2,128,4,512]{3,2,0,1:T(4,128)(2,1)} %copy.33), calls=%async_computation.1 | async-start | bytes 2097152 | tf_op jit(solution)/shard_map/all_to_all | solution.py:58
  70.7 17.6 %while.18 = (s32[]{:T(128)}, f32[2,256,512]{2,1,0:T(8,128)S(1)}, f32[2,256,512]{2,1,0:T(8,128)S(1)}, f32[512,16]{0,1:T(8,128)S(1)}, f32[512,16]{0,1:T(8,128)S(1)...) while((s32[]{:T(128)}, f32[2,256,512]{2,1,0:T(8,128)S(1)}, ...), condition=%wide.region_1.2_spmd.clone.clone.clone, body=%wide.region_0.1_spmd.clone.clone.clone.sunk | while | flops 3682821 | bytes 4242551 | solution.py:95
  71.0 0.8 fusion.161
  72.1 0.8 fusion.161
  73.2 0.8 fusion.161
  74.3 0.8 fusion.161
  75.4 0.8 fusion.161
  76.5 0.8 fusion.161
  77.6 0.8 fusion.161
  78.7 0.8 fusion.161
  79.8 0.8 fusion.161
  80.9 0.8 fusion.161
  82.0 0.8 fusion.161
  83.1 0.8 fusion.161
  84.2 0.8 fusion.161
  85.4 0.8 fusion.161
  86.5 0.8 fusion.161
  87.6 0.8 fusion.161
  88.4 1.4 copy.37
  89.7 1.3 copy.40
  91.2 31.0 %all-to-all-done.1 = bf16[2,128,4,512]{3,2,0,1:T(4,128)(2,1)S(1)} async-done(((bf16[2,128,4,512]{3,2,0,1:T(4,128)(2,1)}), bf16[2,128,4,512]{3,2,0,1:T(4,128)(2,1)S(1)}, u32[]{:S(2)}, u32[]{:S(2)}) %all-to-all-start.1) | async-done | bytes 1048608 | tf_op jit(solution)/shard_map/all_to_all | solution.py:58
  122.3 0.8 copy.57
  124.4 1.6 fusion.39
  126.5 1.6 fusion.37
  128.1 1.6 fusion.15
  129.8 1.8 multiply_subtract_fusion
  131.5 2.0 fusion.33
  133.5 2.0 fusion.35
  135.5 2.0 convolution_add_fusion.1
  137.5 2.4 fusion.20
  140.0 1.1 copy.43
  141.1 75.0 %all_to_all.51 = bf16[2,2,256,512]{3,1,0,2:T(2,128)(2,1)S(1)} all-to-all(bf16[2,2,256,512]{3,1,0,2:T(2,128)(2,1)S(1)} %copy.43), channel_id=1, replica_groups=mesh['ctx'=64,'tp'=8] {'ctx'}, dimensions={2} | all-to-all | bytes 2097152 | tf_op jit(solution)/shard_map/all_to_all | solution.py:110
  219.9 28.3 %all_to_all.52 = bf16[64,4,512]{2,1,0:T(4,128)(2,1)S(1)} all-to-all(bf16[64,4,512]{2,1,0:T(4,128)(2,1)S(1)} %copy.47), channel_id=1, replica_groups=mesh['ctx'=64,'tp'=8] {'ctx'}, dimensions={0} | all-to-all | bytes 524288 | tf_op jit(solution)/shard_map/all_to_all | solution.py:121
  248.3 5.3 %convolution_convert_fusion = bf16[256,4096]{1,0:T(8,128)(2,1)} fusion(bf16[512,4096]{0,1:T(8,128)(2,1)} %all-gather.2.cloned.1.call-done, f32[256,3,512]{2,0,1:T(8,128)} %copy-done, f32[256,512]{1,0:T(8,128)S(1)} %reshape.436, f32[512]{0:T(512)S(1)} %copy-done.5), kind=kOutput, calls=%fused_computation.27 | convolution fusion | flops 1075445760 | bytes 8390656 | tf_op jit(solution)/shard_map/dot_general | solution.py:135
  253.7 34.7 %reduce-scatter.2.cloned.1.call-done = bf16[256,512]{1,0:T(8,128)(2,1)} async-done(((bf16[256,4096]{1,0:T(8,128)(2,1)}), bf16[256,512]{1,0:T(8,128)(2,1)}) %reduce-scatter.2.cloned.1.call-update) | async-done | bytes 262160 | tf_op jit(solution)/shard_map/reduce_scatter | solution.py:140
  (126 shorter events, 13.0 us)
Async XLA Ops:
  7.3 5.1 %collective-permute-start = (bf16[2,3,512]{2,0,1:T(2,128)(2,1)S(1)}, bf16[2,3,512]{2,0,1:T(2,128)(2,1)S(1)}, u32[]{:S(2)}, u32[]{:S(2)}) collective-permute-start(bf16[2,3,512]{2,0,1:T(2,128)(2,1)S(1)} %slice.47), channel_id=1, source_target_pairs={{0,8},{8,16},{16,24},{24,32},{32,40},{40,48},{48,56},{56,64},{64,7... | collective-permute-start | bytes 18440 | tf_op jit(solution)/shard_map/ppermute | solution.py:14
  14.3 1.1 copy-start
  15.5 24.5 %copy-start.3 = (f32[512,16]{0,1:T(8,128)S(1)}, f32[512,16]{0,1:T(8,128)}, u32[]{:S(2)}) copy-start(f32[512,16]{0,1:T(8,128)} %param.11) | copy-start | bytes 98308
  15.5 24.5 %copy-start.4 = (f32[512,16]{0,1:T(8,128)S(1)}, f32[512,16]{0,1:T(8,128)}, u32[]{:S(2)}) copy-start(f32[512,16]{0,1:T(8,128)} %param.10) | copy-start | bytes 98308
  19.5 37.6 %all-to-all-start = ((bf16[64,2,1024]{2,1,0:T(2,128)(2,1)}), bf16[64,2,1024]{2,1,0:T(2,128)(2,1)S(1)}, u32[]{:S(2)}, u32[]{:S(2)}) async-start(bf16[64,2,1024]{2,1,0:T(2,128)(2,1)} %reshape.444), calls=%async_computation | async-start | bytes 524288 | tf_op jit(solution)/shard_map/all_to_all | solution.py:45
  39.1 209.2 %all-gather.2.cloned.1.call-start = ((), (), s32[]{:S(2)}) async-start(), calls=%async_computation.5 | async-start | bytes 4259840 | tf_op jit(solution)/shard_map/all_gather | solution.py:137
  62.5 59.8 %all-to-all-start.1 = ((bf16[2,128,4,512]{3,2,0,1:T(4,128)(2,1)}), bf16[2,128,4,512]{3,2,0,1:T(4,128)(2,1)S(1)}, u32[]{:S(2)}, u32[]{:S(2)}) async-start(bf16[2,128,4,512]{3,2,0,1:T(4,128)(2,1)} %copy.33), calls=%async_computation.1 | async-start | bytes 2097152 | tf_op jit(solution)/shard_map/all_to_all | solution.py:58
  70.5 217.9 %reduce-scatter.2.cloned.1.call-start = ((), (), s32[]{:S(2)}) async-start(), calls=%async_computation.6 | async-start | bytes 2359296 | tf_op jit(solution)/shard_map/reduce_scatter | solution.py:140
  128.1 1.6 copy-start.1
  128.1 1.6 copy-start.2
  219.2 29.1 %copy-start.5 = (f32[512]{0:T(512)S(1)}, f32[512]{0:T(512)}, u32[]{:S(2)}) copy-start(f32[512]{0:T(512)} %param.12) | copy-start | bytes 6148
Sparse Core Ops, SparseCore 0:
  42.8 180.1 all-gather.1
  253.8 34.5 reduce-scatter.1
where the time goes:
time: 297 us; the launch traced here: 295 us
  blocking collectives  103 us (35%)
  waiting for transfers between devices  83.5 us (28%)
  starting transfers between devices  32.2 us (11%)
  matrix products  22.8 us (8%)
  other arithmetic  21.5 us (7%)
  local copies, waits for them, and re-layouts  17.3 us (6%)
  between operations  13.8 us (5%)
    all_to_all x1, blocking collectives, spectral_conv(): lax.all_to_all(for_sending(turned), 'ctx', split_axis=2, concat_axis=1, t...  75 us
    reduce_scatter x1, waiting for transfers between devices, per_device(): lax.psum_scatter(partial_all.astype(jnp.bfloat16), 'tp', scatter_dimensio...  34.7 us
    all_to_all x1, waiting for transfers between devices, spectral_conv(): lax.all_to_all(for_sending(columns_spec), 'ctx', split_axis=1, concat_axi...  31 us
    all_to_all x1, blocking collectives, spectral_conv(): lax.all_to_all(for_sending(signal_cols), 'ctx', split_axis=0, concat_axis...  28.3 us
    all_to_all x1, starting transfers between devices, spectral_conv(): lax.all_to_all(gated_rows[None].astype(jnp.bfloat16), 'ctx', split_axis=1...  19.6 us
    all_to_all x1, waiting for transfers between devices, spectral_conv(): lax.all_to_all(gated_rows[None].astype(jnp.bfloat16), 'ctx', split_axis=1...  17 us
    sub x16, other arithmetic, add_mode(): filt_pair[1] - scale_one * den_im  12.8 us
    all_to_all x1, starting transfers between devices, spectral_conv(): lax.all_to_all(for_sending(columns_spec), 'ctx', split_axis=1, concat_axi...  7.99 us
  transfers between devices with their start and end apart: 5, of which 3 were waited for; matrix products, arithmetic and copies ran while one was open for 16% of the time, Pallas kernels for 0%

commit v1 on v0

v1 whole, which is shorter than its diff:
```python
import functools

import jax
import jax.numpy as jnp
from jax import lax
from jax.experimental import pallas as pl
from jax.experimental.pallas import tpu as pltpu
from jax.sharding import PartitionSpec as P

MESH = pl.DeviceIdType.MESH
F32 = jnp.float32
BF16 = jnp.bfloat16
SUBS = 8


def kernel(
    dims, first_wait, second_wait,
    p_ref, taps_ref, rate_ref, coef_ref, skip_ref, rate_rows_ref, w_ref,
    out_ref,
    gated, query, carry, grow, hid, hidb,
    ends, got_ends, inits, got_inits,
    wall, own, to_pair, from_pair, far, relay_up, relay_dn,
    fin_up, fin_dn, got_up, got_dn,
    sem_e, sem_i, sem_xa, sem_zap, sem_zam, sem_zbp, sem_zbm,
    sem_xbp, sem_xbm, sem_xbr, sem_loc, sem_pair, sem_y,
):
    nx, nz, ny = dims
    n_ctx = nx * nz
    me = lax.axis_index("ctx")
    tp = lax.axis_index("tp")
    x, z = me // nz, me % nz
    y, core = tp // 2, tp % 2
    steps = p_ref.shape[1] - 2
    chans = p_ref.shape[3]
    modes = rate_ref.shape[0]
    groups = chans // 128
    half = 128
    wrows = w_ref.shape[0]
    ra = wrows // 4

    def ctx_id(xx, zz):
        return (lax.rem(xx + nx, nx) * nz + lax.rem(zz + nz, nz), tp)

    def slot(xx, zz):
        return lax.rem(xx + nx, nx) * nz + lax.rem(zz + nz, nz)

    up = (me, lax.rem(y + 1, ny) * 2 + core)
    dn = (me, lax.rem(y + ny - 1, ny) * 2 + core)
    pair = (me, y * 2 + 1 - core)

    barrier = pltpu.get_barrier_semaphore()

    def greet(k, _):
        pl.semaphore_signal(
            barrier, inc=1, device_id=(lax.rem(me + k, n_ctx), tp), device_id_type=MESH
        )
        return 0

    lax.fori_loop(1, n_ctx, greet, 0)
    for other in (up, dn, pair):
        pl.semaphore_signal(barrier, inc=1, device_id=other, device_id_type=MESH)

    mine = pltpu.make_async_copy(w_ref, wall.at[me], sem_loc.at[0])
    mine.start()

    sub = lax.broadcasted_iota(jnp.int32, (SUBS, 128), 0)
    for q in range(groups):
        lanes = pl.ds(q * 128, 128)

        def row(ref, *idx):
            return jnp.broadcast_to(ref[(*idx, pl.ds(0, 1), lanes)], (SUBS, 128))

        taps = [[row(taps_ref, i, s) for i in range(3)] for s in range(3)]
        decay = [jnp.exp(-row(rate_ref, r)) for r in range(modes)]

        def first_pass(j, state):
            def mixed(s):
                t = taps[s]
                return (
                    t[0] * p_ref[s, j + 2, :, lanes]
                    + t[1] * p_ref[s, j + 1, :, lanes]
                    + t[2] * p_ref[s, j, :, lanes]
                )

            value = mixed(1) * mixed(2)
            gated[j, :, lanes] = value
            query[j, :, lanes] = mixed(0)
            return tuple(decay[r] * state[r] + value for r in range(modes))

        zero = jnp.zeros((SUBS, 128), F32)
        state = lax.fori_loop(0, steps, first_pass, (zero,) * modes, unroll=2)
        for r in range(modes):
            rate = row(rate_ref, r)
            total = state[r]
            for gap in (1, 2, 4):
                moved = jnp.where(sub >= gap, pltpu.roll(total, gap, 0), 0.0)
                total = total + jnp.exp(-(float(steps * gap)) * rate) * moved
            ends[r * groups + q] = total[SUBS - 1:, :]
            carry[r, :, lanes] = jnp.where(sub >= 1, pltpu.roll(total, 1, 0), 0.0)
            grow[r, :, lanes] = jnp.exp(-float(steps) * sub.astype(F32) * rate)

    pl.semaphore_wait(barrier, n_ctx - 1 + 3)

    pending = []

    def remote(src, dst, send, recv, dev):
        return pltpu.make_async_remote_copy(
            src_ref=src, dst_ref=dst, send_sem=send, recv_sem=recv,
            device_id=dev, device_id_type=MESH,
        )

    def exchange(src, dst, sems):
        def one(k):
            other = lax.rem(me + k, n_ctx)
            return remote(
                src.at[other], dst.at[me], sems.at[0, k], sems.at[1, k], (other, tp)
            )

        def come(k):
            other = lax.rem(me - k + n_ctx, n_ctx)
            return remote(
                src.at[other], dst.at[other], sems.at[0, k], sems.at[1, k], (other, tp)
            )

        def go(k, _):
            one(k).start()
            return 0

        def done(k, _):
            come(k).wait_recv()
            return 0

        def sent(k, _):
            one(k).wait_send()
            return 0

        return (
            lambda: lax.fori_loop(1, n_ctx, go, 0),
            lambda: lax.fori_loop(1, n_ctx, done, 0),
            lambda: lax.fori_loop(1, n_ctx, sent, 0),
        )

    go_ends, wait_ends, sent_ends = exchange(ends, got_ends, sem_e)
    go_inits, wait_inits, sent_inits = exchange(inits, got_inits, sem_i)
    go_ends()
    got_ends[me] = ends[me]

    lo, hi = pl.ds(0, ra), pl.ds(ra, wrows - ra)

    def w_copy(part, xx, zz, sems, idx, dev, own_src=False):
        at = wall.at[slot(xx, zz), part]
        src = w_ref.at[part] if own_src else at
        return remote(src, at, sems.at[(0, *idx)], sems.at[(1, *idx)], dev)

    def start(copy):
        copy.start()
        pending.append(copy)

    ring = nz // 2
    z_up, z_dn = ctx_id(x, z + 1), ctx_id(x, z - 1)
    x_up, x_dn = ctx_id(x + 1, z), ctx_id(x - 1, z)

    def send_ap(s, dx):
        start(w_copy(lo, x + dx, z - s + 1, sem_zap, (s, dx), z_up, s == 1 and dx == 0))

    def send_am(s, dx):
        start(w_copy(lo, x + dx, z + s - 1, sem_zam, (s, dx), z_dn, s == 1 and dx == 0))

    def send_bp(s):
        start(w_copy(hi, x, z - s + 1, sem_zbp, (s,), z_up, s == 1))

    def send_bm(s):
        start(w_copy(hi, x, z + s - 1, sem_zbm, (s,), z_dn, s == 1))

    def send_bx(e):
        start(w_copy(hi, x, z + e, sem_xbp, (e % nz,), x_up, e == 0))
        start(w_copy(hi, x, z + e, sem_xbm, (e % nz,), x_dn, e == 0))

    def relay_bx(e):
        w_copy(hi, x - 1, z + e, sem_xbp, (e % nz,), x_up).wait_recv()
        w_copy(hi, x + 1, z + e, sem_xbm, (e % nz,), x_dn).wait_recv()
        if e % 2 == 0:
            start(w_copy(hi, x - 1, z + e, sem_xbr, (e % nz,), x_up))
        else:
            start(w_copy(hi, x + 1, z + e, sem_xbr, (e % nz,), x_dn))

    send_ap(1, 0)
    send_am(1, 0)
    send_bp(1)
    send_bm(1)
    for dx in range(1, nx):
        start(w_copy(lo, x, z, sem_xa, (dx,), ctx_id(x + dx, z), True))
    send_bx(0)
    for dx in range(1, nx):
        w_copy(lo, x + dx, z, sem_xa, (nx - dx,), x_up).wait_recv()
        send_ap(1, dx)
        send_am(1, dx)

    def ring_step(s):
        w_copy(hi, x, z - s, sem_zbp, (s,), z_up).wait_recv()
        if s < ring:
            send_bp(s + 1)
        send_bx(-s)
        if s < ring:
            w_copy(hi, x, z + s, sem_zbm, (s,), z_dn).wait_recv()
            if s < ring - 1:
                send_bm(s + 1)
            send_bx(s)
        for dx in range(nx):
            w_copy(lo, x + dx, z - s, sem_zap, (s, dx), z_up).wait_recv()
            if s < ring:
                send_ap(s + 1, dx)
                w_copy(lo, x + dx, z + s, sem_zam, (s, dx), z_dn).wait_recv()
                if s < ring - 1:
                    send_am(s + 1, dx)
        relay_bx(-(s - 1))
        if s > 1:
            relay_bx(s - 1)

    def prefix():
        wait_ends()
        leap = jnp.exp(-float(steps * SUBS) * rate_rows_ref[me])

        def body(p, state):
            inits[p] = state
            return leap * state + got_ends[p]

        lax.fori_loop(0, n_ctx, body, jnp.zeros((1, 128), F32), unroll=4)
        go_inits()
        got_inits[me] = inits[me]

    def finish_conv():
        wait_inits()
        for q in range(groups):
            lanes = pl.ds(q * 128, 128)

            def row(ref, *idx):
                return jnp.broadcast_to(ref[(*idx, pl.ds(0, 1), lanes)], (SUBS, 128))

            decay = [jnp.exp(-row(rate_ref, r)) for r in range(modes)]
            coef = [row(coef_ref, r) for r in range(modes)]
            skip = row(skip_ref)

            def second_pass(j, state):
                value = gated[j, :, lanes]
                after = tuple(decay[r] * state[r] + value for r in range(modes))
                terms = [coef[r] * after[r] for r in range(modes)] + [skip * value]
                while len(terms) > 1:
                    rest = terms[len(terms) // 2 * 2:]
                    terms = [a + b for a, b in zip(terms[::2], terms[1::2])] + rest
                hid[j, :, lanes] = query[j, :, lanes] * terms[0]
                return after

            begin = tuple(
                carry[r, :, lanes]
                + grow[r, :, lanes] * jnp.broadcast_to(got_inits[r * groups + q], (SUBS, 128))
                for r in range(modes)
            )
            lax.fori_loop(0, steps, second_pass, begin, unroll=2)
        hidb[...] = hid[...].reshape(steps * SUBS, chans).astype(BF16)

    for s in range(1, ring + 1):
        if s == first_wait:
            prefix()
        if s == second_wait:
            finish_conv()
        ring_step(s)
    relay_bx(-ring)
    for e in range(nz):
        w_copy(hi, x + 2, z + e, sem_xbr, (e,), x_up).wait_recv()
    mine.wait()

    per = n_ctx // (2 * ny)

    def project(yy, cc):
        at = pl.multiple_of((yy * 2 + cc) * per, per)
        block = wall[pl.ds(at, per)].reshape(per * wrows, chans)
        return lax.dot_general(
            hidb[...], block, (((1,), (1,)), ((), ())), preferred_element_type=F32
        )

    order = [2, 1, ny - 1, 0]

    def pair_copy(i):
        return remote(to_pair.at[i], from_pair.at[i], sem_pair.at[0, i], sem_pair.at[1, i], pair)

    for i, dy in enumerate(order):
        to_pair[i] = project(lax.rem(y + dy, ny), 1 - core).astype(BF16)
        start(pair_copy(i))
    for i, dy in enumerate(order):
        own[i] = project(lax.rem(y + dy, ny), core)

    def top(ref):
        return ref.at[pl.ds(0, half)]

    def bottom(ref):
        return ref.at[pl.ds(half, half)]

    def y_copy(src, dst, k, dev):
        return remote(src, dst, sem_y.at[0, k], sem_y.at[1, k], dev)

    far_up = y_copy(top(far), relay_up, 0, up)
    far_dn = y_copy(bottom(far), relay_dn, 1, dn)
    up_bottom = y_copy(bottom(fin_up), bottom(got_up), 2, up)
    dn_top = y_copy(top(fin_dn), top(got_dn), 3, dn)
    up_top = y_copy(top(fin_up), top(got_up), 4, up)
    dn_bottom = y_copy(bottom(fin_dn), bottom(got_dn), 5, dn)
    hi_rows, lo_rows = pl.ds(0, half), pl.ds(half, half)

    pair_copy(0).wait_recv()
    far[...] = (own[0] + from_pair[0].astype(F32)).astype(BF16)
    start(far_up)
    start(far_dn)
    pair_copy(1).wait_recv()
    fin_up[lo_rows] = (own[1, lo_rows] + from_pair[1, lo_rows].astype(F32)).astype(BF16)
    start(up_bottom)
    pair_copy(2).wait_recv()
    fin_dn[hi_rows] = (own[2, hi_rows] + from_pair[2, hi_rows].astype(F32)).astype(BF16)
    start(dn_top)
    far_up.wait_recv()
    fin_up[hi_rows] = (
        own[1, hi_rows] + from_pair[1, hi_rows].astype(F32) + relay_up[...].astype(F32)
    ).astype(BF16)
    start(up_top)
    far_dn.wait_recv()
    fin_dn[lo_rows] = (
        own[2, lo_rows] + from_pair[2, lo_rows].astype(F32) + relay_dn[...].astype(F32)
    ).astype(BF16)
    start(dn_bottom)
    pair_copy(3).wait_recv()
    own[3] = own[3] + from_pair[3].astype(F32)
    up_bottom.wait_recv()
    dn_top.wait_recv()
    up_top.wait_recv()
    dn_bottom.wait_recv()
    out_ref[...] = (own[3] + got_up[...].astype(F32) + got_dn[...].astype(F32)).astype(BF16)

    sent_ends()
    sent_inits()
    for copy in pending:
        copy.wait_send()


def per_device(dims, projected, short_filter, residues, rates, skip_gain, out_weight):
    nx, nz, ny = dims
    n_ctx = nx * nz
    rows, _, chans = projected.shape
    modes = rates.shape[1]
    steps = rows // SUBS
    groups = chans // 128
    wrows = out_weight.shape[1]
    earlier = lax.ppermute(projected[-2:], "ctx", [(i, i + 1) for i in range(n_ctx - 1)])
    padded = jnp.concatenate([earlier, projected], axis=0)
    windows = jnp.stack([padded[k * steps:k * steps + steps + 2] for k in range(SUBS)], axis=0)
    laid = windows.transpose(2, 1, 0, 3).astype(F32)
    coef = (residues * jnp.sqrt(-jnp.expm1(-2.0 * rates))).T
    rate_t = rates.T
    dma = pltpu.SemaphoreType.DMA
    vm = pltpu.VMEM
    ring = nz // 2
    out = pl.pallas_call(
        functools.partial(kernel, dims, 3, 6),
        out_shape=jax.ShapeDtypeStruct((rows, chans), BF16),
        in_specs=[pl.BlockSpec(memory_space=pltpu.VMEM)] * 7,
        out_specs=pl.BlockSpec(memory_space=pltpu.VMEM),
        scratch_shapes=[
            vm((steps, SUBS, chans), F32),
            vm((steps, SUBS, chans), F32),
            vm((modes, SUBS, chans), F32),
            vm((modes, SUBS, chans), F32),
            vm((steps, SUBS, chans), F32),
            vm((rows, chans), BF16),
            vm((n_ctx, 1, 128), F32),
            vm((n_ctx, 1, 128), F32),
            vm((n_ctx, 1, 128), F32),
            vm((n_ctx, 1, 128), F32),
            vm((n_ctx, wrows, chans), BF16),
            vm((ny, rows, chans), F32),
            vm((ny, rows, chans), BF16),
            vm((ny, rows, chans), BF16),
            vm((rows, chans), BF16),
            vm((rows // 2, chans), BF16),
            vm((rows // 2, chans), BF16),
            vm((rows, chans), BF16),
            vm((rows, chans), BF16),
            vm((rows, chans), BF16),
            vm((rows, chans), BF16),
            dma((2, n_ctx)),
            dma((2, n_ctx)),
            dma((2, nx)),
            dma((2, ring + 1, nx)),
            dma((2, ring + 1, nx)),
            dma((2, ring + 1)),
            dma((2, ring + 1)),
            dma((2, nz)),
            dma((2, nz)),
            dma((2, nz)),
            dma((1,)),
            dma((2, ny)),
            dma((2, 6)),
        ],
        compiler_params=pltpu.CompilerParams(
            collective_id=0, has_side_effects=True, vmem_limit_bytes=48 * 1024 * 1024
        ),
    )(
        laid,
        short_filter[:, :, None, :],
        rate_t[:, None, :],
        coef[:, None, :],
        skip_gain[None, :],
        rate_t.reshape(modes * groups, 1, 128),
        out_weight.T,
    )
    return out.reshape(steps, SUBS, chans).transpose(1, 0, 2).reshape(rows, chans)


def solution(mesh):
    dims = (4, mesh.shape["ctx"] // 4, mesh.shape["tp"] // 2)
    return jax.shard_map(
        functools.partial(per_device, dims),
        mesh=mesh,
        in_specs=(
            P("ctx", None, "tp"),
            P(None, None, "tp"),
            P("tp", None),
            P("tp", None),
            P("tp"),
            P("tp", "ctx"),
        ),
        out_specs=P("ctx", "tp"),
        check_vma=False,
    )
```

time: 297 us -> 94.2 us (0.32)
  blocking collectives: 103 us -> 0 us
  waiting for transfers between devices: 83.5 us -> 0.01 us
  Pallas kernels: 0 us -> 74.9 us
  starting transfers between devices: 32.2 us -> 4.36 us
  matrix products: 22.8 us -> 0 us
  other arithmetic: 21.5 us -> 2.77 us
  between operations: 13.8 us -> 0.15 us
  local copies, waits for them, and re-layouts: 17.3 us -> 11.5 us
    all_to_all x2 -> x0, blocking collectives: 103 us -> none  [the longest x1 75 us: spectral_conv(): lax.all_to_all(for_sending(turned), 'ctx', split_axis=2, concat_axis=1, t...]
    pallas_call x0 -> x1, Pallas kernels: none -> 74.9 us  [per_device(): pl.pallas_call(functools.partial(kernel, dims, 3, 6), out_shape=jax.Shape...]
    all_to_all x2 -> x0, waiting for transfers between devices: 48.1 us -> none  [the longest x1 31 us: spectral_conv(): lax.all_to_all(for_sending(columns_spec), 'ctx', split_axis=1, concat_axi...]
    reduce_scatter x1 -> x0, waiting for transfers between devices: 34.7 us -> none  [per_device(): lax.psum_scatter(partial_all.astype(jnp.bfloat16), 'tp', scatter_dimensio...]
    all_to_all x2 -> x0, starting transfers between devices: 27.5 us -> none  [the longest x1 19.6 us: spectral_conv(): lax.all_to_all(gated_rows[None].astype(jnp.bfloat16), 'ctx', split_axis=1...]
    dot_general x13 -> x0, matrix products: 22.8 us -> none  [the longest x1 5.35 us: per_device(): jnp.dot(hidden, lax.all_gather(out_weight, 'ctx', axis=1, tiled=True), pr...]
    sub x16 -> x0, other arithmetic: 12.8 us -> none  [add_mode(): filt_pair[1] - scale_one * den_im]
    another operation x2 -> x9, local copies, waits for them, and re-layouts: 2.9 us -> 7 us  [per_device(): jnp.stack([padded[k * steps:k * steps + steps + 2] for k in range(SUBS)],...]
  transfers between devices with their start and end apart: 5 -> 1, of which waited for: 3 -> 0; matrix products, arithmetic and copies ran while one was open for 16% -> 3% of each run, Pallas kernels for 0% -> 0%
where the time goes in v1:
time: 94.2 us; the launch traced here: 93.7 us
  Pallas kernels  74.9 us (80%)
  local copies, waits for them, and re-layouts  11.5 us (12%)
  starting transfers between devices  4.36 us (5%)
  other arithmetic  2.77 us (3%)
    pallas_call x1, Pallas kernels, per_device(): pl.pallas_call(functools.partial(kernel, dims, 3, 6), out_shape=jax.Shape...  74.9 us
    another operation x9, local copies, waits for them, and re-layouts, per_device(): jnp.stack([padded[k * steps:k * steps + steps + 2] for k in range(SUBS)],...  7 us
    ppermute x1, starting transfers between devices, per_device(): lax.ppermute(projected[-2:], 'ctx', [(i, i + 1) for i in range(n_ctx - 1)])  4.36 us
  transfers between devices with their start and end apart: 1, of which 0 were waited for; matrix products, arithmetic and copies ran while one was open for 3% of the time, Pallas kernels for 0%

profile of v1, /device:TPU:1, one launch (start us, length us, event | category | flops | bytes accessed | tf_op | source)
XLA Modules:
  0.0 93.7 jit_solution(17524350267457621836)
XLA Ops:
  0.0 0.7 slice.27
  0.8 4.4 %collective-permute-start = (bf16[2,3,512]{2,0,1:T(2,128)(2,1)S(1)}, bf16[2,3,512]{2,0,1:T(2,128)(2,1)S(1)}, u32[]{:S(2)}, u32[]{:S(2)}) collective-permute-start(bf16[2,3,512]{2,0,1:T(2,128)(2,1)S(1)} %slice.27), channel_id=1, source_target_pairs={{0,8},{8,16},{16,24},{24,32},{32,40},{40,48},{48,56},{56,64},{64,7... | collective-permute-start | bytes 18440 | tf_op jit(solution)/shard_map/ppermute | solution.py:352
  5.1 0.8 multiply_bitcast_fusion
  5.9 0.8 broadcast_in_dim.13.rate_ref
  6.7 0.8 reshape.9.rate_rows_ref
  7.5 0.8 broadcast_in_dim.12.taps_ref
  8.3 0.0 collective-permute-done
  8.3 1.8 %slice_bitcast_fusion = (bf16[1,34,3,512]{3,1,2,0:T(8,128)(2,1)S(1)}, bf16[1,34,3,512]{3,1,2,0:T(8,128)(2,1)S(1)}, bf16[1,34,3,512]{3,1,2,0:T(8,128)(2,1)S(1)}, ...) fusion(bf16[256,3,512]{2,0,1:T(8,128)(2,1)} %param.6, ...), kind=kLoop, calls=%fused_computation.3 | loop fusion | flops 208896 | bytes 2488320 | tf_op jit(solution)/shard_map/stack | solution.py:354
  10.1 0.2 copy.10
  10.2 0.2 copy.11
  10.4 0.2 copy.12
  10.6 0.2 copy.13
  10.8 0.2 copy.14
  10.9 0.2 copy.15
  11.1 0.2 copy.8
  11.3 0.2 copy.9
  11.4 5.7 %stack.35 = bf16[8,34,3,512]{3,0,1,2:T(8,128)(2,1)S(1)} concatenate(bf16[1,34,3,512]{3,0,1,2:T(2,128)(2,1)S(1)} %copy.8, bf16[1,34,3,512]{3,0,1,2:T(2,128)(2,1)S(1)} %copy.9, bf16[1,34,3,512]{3,0,1,2:T(2,128)(2,1)S(1)} %copy.10, bf16[1,34,3,512]{3,0,1,2:T(2,128)(2,1)S(1)} %copy.11, bf16[1,34,3,512]{3,0,1,2:T(2,128)(2,1)S(1)} %copy.12, bf16[1,34,3,512]{3,0,1,2:T(2,128)(2,1)S(1)} %copy.13, ...), dimensions={0} | concatenate | bytes 1671168 | tf_op jit(solution)/shard_map/stack | solution.py:354
  17.1 0.0 copy-start
  17.2 0.0 copy-start.1
  17.2 0.2 convert_bitcast_fusion.p_ref
  17.4 0.6 copy-done
  18.0 0.0 copy-done.1
  18.0 74.9 %shard_map.64 = bf16[256,512]{1,0:T(8,128)(2,1)S(1)} custom-call(f32[3,34,8,512]{3,2,1,0:T(8,128)S(1)} %convert_bitcast_fusion.p_ref, f32[3,3,1,512]{3,2,1,0:T(1,128)S(1)} %broadcast_in_dim.12.taps_ref, f32[16,1,512]{2,1,0:T(1,128)S(1)} %broadcast_in_dim.13.rate_ref, f32[16,1,512]{2,1,0:T(1,128)S(1)} %broadcast_in_dim.14.coef_ref, f32[1,512]{1,0:T(1,128)S(1)} %bitcast.29, ...), custom_call_target="tpu_custom_call" | custom-call | tf_op jit(solution)/shard_map/pallas_call | solution.py:361
  92.9 0.8 copy.16
  (1 shorter events, 0.0 us)
Async XLA Ops:
  0.8 7.6 %collective-permute-start = (bf16[2,3,512]{2,0,1:T(2,128)(2,1)S(1)}, bf16[2,3,512]{2,0,1:T(2,128)(2,1)S(1)}, u32[]{:S(2)}, u32[]{:S(2)}) collective-permute-start(bf16[2,3,512]{2,0,1:T(2,128)(2,1)S(1)} %slice.27), channel_id=1, source_target_pairs={{0,8},{8,16},{16,24},{24,32},{32,40},{40,48},{48,56},{56,64},{64,7... | collective-permute-start | bytes 18440 | tf_op jit(solution)/shard_map/ppermute | solution.py:352
  17.1 0.8 copy-start
  17.2 0.8 copy-start.1

commit v2 on v1

--- a/solution.py
+++ b/solution.py
@@ -11,18 +11,21 @@
 F32 = jnp.float32
 BF16 = jnp.bfloat16
 SUBS = 8
+FIRST, SECOND, SPLIT = 5, 9, 16
 
 
 def kernel(
-    dims, first_wait, second_wait,
-    p_ref, taps_ref, rate_ref, coef_ref, skip_ref, rate_rows_ref, w_ref,
+    dims, first_wait, second_wait, ra,
+    p_in, taps_in, rate_in, res_in, skip_in, w_in,
     out_ref,
-    gated, query, carry, grow, hid, hidb,
+    p_ref, taps_ref, rate_ref, res_ref, skip_ref, w_ref,
+    pf, tail, coef_ref, leaps, gated, query, carry, grow, hid, hidb,
     ends, got_ends, inits, got_inits,
     wall, own, to_pair, from_pair, far, relay_up, relay_dn,
     fin_up, fin_dn, got_up, got_dn,
     sem_e, sem_i, sem_xa, sem_zap, sem_zam, sem_zbp, sem_zbm,
-    sem_xbp, sem_xbm, sem_xbr, sem_loc, sem_pair, sem_y,
+    sem_xbp, sem_xbm, sem_xbr, sem_loc, sem_pair, sem_y, sem_tail,
+    sem_r1, sem_r2, sem_r3, sem_r4,
 ):
     nx, nz, ny = dims
     n_ctx = nx * nz
@@ -30,13 +33,12 @@
     tp = lax.axis_index("tp")
     x, z = me // nz, me % nz
     y, core = tp // 2, tp % 2
-    steps = p_ref.shape[1] - 2
-    chans = p_ref.shape[3]
+    steps = p_ref.shape[1] // SUBS
+    chans = p_ref.shape[2]
     modes = rate_ref.shape[0]
     groups = chans // 128
     half = 128
     wrows = w_ref.shape[0]
-    ra = wrows // 4
 
     def ctx_id(xx, zz):
         return (lax.rem(xx + nx, nx) * nz + lax.rem(zz + nz, nz), tp)
@@ -48,58 +50,38 @@
     dn = (me, lax.rem(y + ny - 1, ny) * 2 + core)
     pair = (me, y * 2 + 1 - core)
 
+    loads = [
+        pltpu.make_async_copy(src, dst, sem_loc.at[i])
+        for i, (src, dst) in enumerate((
+            (w_in, w_ref), (p_in, p_ref), (taps_in, taps_ref), (rate_in, rate_ref),
+            (res_in, res_ref), (skip_in, skip_ref), (w_in, wall.at[me]),
+        ))
+    ]
+    for load in loads:
+        load.start()
+
     barrier = pltpu.get_barrier_semaphore()
 
-    def greet(k, _):
-        pl.semaphore_signal(
-            barrier, inc=1, device_id=(lax.rem(me + k, n_ctx), tp), device_id_type=MESH
-        )
-        return 0
-
-    lax.fori_loop(1, n_ctx, greet, 0)
-    for other in (up, dn, pair):
+    near = [(lax.rem(x + dx, nx) * nz + z, tp) for dx in range(1, nx)]
+    near += [(x * nz + lax.rem(z + dz, nz), tp) for dz in (1, nz - 1)]
+    near += [up, dn, pair]
+    for other in near:
         pl.semaphore_signal(barrier, inc=1, device_id=other, device_id_type=MESH)
 
-    mine = pltpu.make_async_copy(w_ref, wall.at[me], sem_loc.at[0])
-    mine.start()
-
-    sub = lax.broadcasted_iota(jnp.int32, (SUBS, 128), 0)
-    for q in range(groups):
-        lanes = pl.ds(q * 128, 128)
-
-        def row(ref, *idx):
-            return jnp.broadcast_to(ref[(*idx, pl.ds(0, 1), lanes)], (SUBS, 128))
-
-        taps = [[row(taps_ref, i, s) for i in range(3)] for s in range(3)]
-        decay = [jnp.exp(-row(rate_ref, r)) for r in range(modes)]
-
-        def first_pass(j, state):
-            def mixed(s):
-                t = taps[s]
-                return (
-                    t[0] * p_ref[s, j + 2, :, lanes]
-                    + t[1] * p_ref[s, j + 1, :, lanes]
-                    + t[2] * p_ref[s, j, :, lanes]
-                )
-
-            value = mixed(1) * mixed(2)
-            gated[j, :, lanes] = value
-            query[j, :, lanes] = mixed(0)
-            return tuple(decay[r] * state[r] + value for r in range(modes))
-
-        zero = jnp.zeros((SUBS, 128), F32)
-        state = lax.fori_loop(0, steps, first_pass, (zero,) * modes, unroll=2)
-        for r in range(modes):
-            rate = row(rate_ref, r)
-            total = state[r]
-            for gap in (1, 2, 4):
-                moved = jnp.where(sub >= gap, pltpu.roll(total, gap, 0), 0.0)
-                total = total + jnp.exp(-(float(steps * gap)) * rate) * moved
-            ends[r * groups + q] = total[SUBS - 1:, :]
-            carry[r, :, lanes] = jnp.where(sub >= 1, pltpu.roll(total, 1, 0), 0.0)
-            grow[r, :, lanes] = jnp.exp(-float(steps) * sub.astype(F32) * rate)
-
-    pl.semaphore_wait(barrier, n_ctx - 1 + 3)
+    rows = steps * SUBS
+    for load in loads:
+        load.wait()
+    twice = 2.0 * rate_ref[...]
+    small = jnp.ones_like(twice)
+    for k in range(9, 1, -1):
+        small = 1.0 - small * twice * (1.0 / k)
+    lost = jnp.where(twice < 0.25, twice * small, 1.0 - jnp.exp(-twice))
+    coef_ref[...] = res_ref[...] * jnp.sqrt(lost)
+    for s in range(3):
+        for q in range(groups):
+            pf[s, q, pl.ds(8, rows), :] = p_ref[s, :, pl.ds(q * 128, 128)].astype(F32)
+
+    pl.semaphore_wait(barrier, len(near))
 
     pending = []
 
@@ -139,11 +121,6 @@
             lambda: lax.fori_loop(1, n_ctx, done, 0),
             lambda: lax.fori_loop(1, n_ctx, sent, 0),
         )
-
-    go_ends, wait_ends, sent_ends = exchange(ends, got_ends, sem_e)
-    go_inits, wait_inits, sent_inits = exchange(inits, got_inits, sem_i)
-    go_ends()
-    got_ends[me] = ends[me]
 
     lo, hi = pl.ds(0, ra), pl.ds(ra, wrows - ra)
 
@@ -217,9 +194,108 @@
         if s > 1:
             relay_bx(s - 1)
 
+    go_ends, wait_ends, sent_ends = exchange(ends, got_ends, sem_e)
+    go_inits, wait_inits, sent_inits = exchange(inits, got_inits, sem_i)
+
+
+    def herald(sem, gap):
+        for dz in (gap, nz - gap):
+            pl.semaphore_signal(
+                sem, inc=1, device_id=(x * nz + lax.rem(z + dz, nz), tp), device_id_type=MESH
+            )
+
+    def row(ref, at, lanes):
+        return jnp.broadcast_to(ref[pl.ds(at, 1), lanes], (SUBS, 128))
+
+    sub = lax.broadcasted_iota(jnp.int32, (SUBS, 128), 0)
+
+    def mixer(q):
+        lanes = pl.ds(q * 128, 128)
+        taps = [
+            [jnp.broadcast_to(taps_ref[i, pl.ds(s, 1), lanes], (SUBS, 128)) for i in range(3)]
+            for s in range(3)
+        ]
+
+        def mixed(s, j):
+            return sum(
+                taps[s][i] * pf[s, q, pl.ds(8 + j - i, SUBS, stride=steps), :] for i in range(3)
+            )
+
+        def at_step(j):
+            value = mixed(1, j) * mixed(2, j)
+            gated[j, :, lanes] = value
+            query[j, :, lanes] = mixed(0, j)
+            return value
+
+        return at_step
+
+    def first_pass(q):
+        lanes = pl.ds(q * 128, 128)
+        decay = [jnp.exp(-row(rate_ref, r, lanes)) for r in range(modes)]
+        at_step = mixer(q)
+
+        def body(j, state):
+            value = at_step(j)
+            return tuple(decay[r] * state[r] + value for r in range(modes))
+
+        zero = jnp.zeros((SUBS, 128), F32)
+        state = lax.fori_loop(2, steps, body, (zero,) * modes, unroll=2)
+        for r in range(modes):
+            carry[r, :, lanes] = state[r]
+            grow[r, :, lanes] = jnp.exp(
+                -float(steps) * sub.astype(F32) * row(rate_ref, r, lanes)
+            )
+
+    def first_steps(q):
+        lanes = pl.ds(q * 128, 128)
+        for s in range(3):
+            edge = tail[s, :, lanes].astype(F32)
+            pf[s, q, pl.ds(0, 8), :] = jnp.where(me > 0, edge, 0.0)
+        at_step = mixer(q)
+        zeroth = at_step(0)
+        first = at_step(1)
+        for r in range(modes):
+            rate = row(rate_ref, r, lanes)
+            total = (
+                carry[r, :, lanes]
+                + jnp.exp(-float(steps - 1) * rate) * zeroth
+                + jnp.exp(-float(steps - 2) * rate) * first
+            )
+            for gap in (1, 2, 4):
+                moved = jnp.where(sub >= gap, pltpu.roll(total, gap, 0), 0.0)
+                total = total + jnp.exp(-(float(steps * gap)) * rate) * moved
+            ends[r * groups + q] = total[SUBS - 1:, :]
+            leaps[r * groups + q] = jnp.exp(-float(rows) * rate[:1])
+            carry[r, :, lanes] = jnp.where(sub >= 1, pltpu.roll(total, 1, 0), 0.0)
+
+    herald(sem_r1, 1)
+    first_pass(0)
+    pl.semaphore_wait(sem_r1, 2)
+    herald(sem_r2, 2)
+    send_tail = remote(
+        p_ref.at[:, pl.ds(rows - 8, 8)], tail, sem_tail.at[0], sem_tail.at[1],
+        (lax.rem(me + 1, n_ctx), tp),
+    )
+    start(send_tail)
+    first_pass(1)
+    pl.semaphore_wait(sem_r2, 2)
+    herald(sem_r3, 4)
+    for q in range(2, groups):
+        first_pass(q)
+    send_tail.wait_recv()
+    for q in range(groups):
+        first_steps(q)
+    pl.semaphore_wait(sem_r3, 2)
+    herald(sem_r4, 1)
+
+    def depart():
+        pl.semaphore_wait(sem_r4, 2)
+        go_ends()
+        got_ends[me] = ends[me]
+
     def prefix():
         wait_ends()
-        leap = jnp.exp(-float(steps * SUBS) * rate_rows_ref[me])
+        leap = leaps[me]
 
         def body(p, state):
             inits[p] = state
@@ -234,12 +310,9 @@
         for q in range(groups):
             lanes = pl.ds(q * 128, 128)
 
-            def row(ref, *idx):
-                return jnp.broadcast_to(ref[(*idx, pl.ds(0, 1), lanes)], (SUBS, 128))
-
-            decay = [jnp.exp(-row(rate_ref, r)) for r in range(modes)]
-            coef = [row(coef_ref, r) for r in range(modes)]
-            skip = row(skip_ref)
+            decay = [jnp.exp(-row(rate_ref, r, lanes)) for r in range(modes)]
+            coef = [row(coef_ref, r, lanes) for r in range(modes)]
+            skip = row(skip_ref, 0, lanes)
 
             def second_pass(j, state):
                 value = gated[j, :, lanes]
@@ -259,16 +332,18 @@
             lax.fori_loop(0, steps, second_pass, begin, unroll=2)
         hidb[...] = hid[...].reshape(steps * SUBS, chans).astype(BF16)
 
-    for s in range(1, ring + 1):
+    for s in range(1, ring + 2):
+        if s == 2:
+            depart()
         if s == first_wait:
             prefix()
         if s == second_wait:
             finish_conv()
-        ring_step(s)
+        if s <= ring:
+            ring_step(s)
     relay_bx(-ring)
     for e in range(nz):
         w_copy(hi, x + 2, z + e, sem_xbr, (e,), x_up).wait_recv()
-    mine.wait()
 
     per = n_ctx // (2 * ny)
 
@@ -349,21 +424,26 @@
     steps = rows // SUBS
     groups = chans // 128
     wrows = out_weight.shape[1]
-    earlier = lax.ppermute(projected[-2:], "ctx", [(i, i + 1) for i in range(n_ctx - 1)])
-    padded = jnp.concatenate([earlier, projected], axis=0)
-    windows = jnp.stack([padded[k * steps:k * steps + steps + 2] for k in range(SUBS)], axis=0)
-    laid = windows.transpose(2, 1, 0, 3).astype(F32)
-    coef = (residues * jnp.sqrt(-jnp.expm1(-2.0 * rates))).T
     rate_t = rates.T
     dma = pltpu.SemaphoreType.DMA
     vm = pltpu.VMEM
     ring = nz // 2
     out = pl.pallas_call(
-        functools.partial(kernel, dims, 3, 6),
+        functools.partial(kernel, dims, FIRST, SECOND, SPLIT),
         out_shape=jax.ShapeDtypeStruct((rows, chans), BF16),
-        in_specs=[pl.BlockSpec(memory_space=pltpu.VMEM)] * 7,
+        in_specs=[pl.BlockSpec(memory_space=pltpu.HBM)] * 6,
         out_specs=pl.BlockSpec(memory_space=pltpu.VMEM),
         scratch_shapes=[
+            vm((3, rows, chans), BF16),
+            vm((3, 3, chans), F32),
+            vm((modes, chans), F32),
+            vm((modes, chans), F32),
+            vm((1, chans), F32),
+            vm((wrows, chans), BF16),
+            vm((3, groups, rows + 8, 128), F32),
+            vm((3, 8, chans), BF16),
+            vm((modes, chans), F32),
+            vm((n_ctx, 1, 128), F32),
             vm((steps, SUBS, chans), F32),
             vm((steps, SUBS, chans), F32),
             vm((modes, SUBS, chans), F32),
@@ -395,20 +475,24 @@
             dma((2, nz)),
             dma((2, nz)),
             dma((2, nz)),
-            dma((1,)),
+            dma((7,)),
             dma((2, ny)),
             dma((2, 6)),
+            dma((2,)),
+            pltpu.SemaphoreType.REGULAR,
+            pltpu.SemaphoreType.REGULAR,
+            pltpu.SemaphoreType.REGULAR,
+            pltpu.SemaphoreType.REGULAR,
         ],
         compiler_params=pltpu.CompilerParams(
-            collective_id=0, has_side_effects=True, vmem_limit_bytes=48 * 1024 * 1024
+            collective_id=0, has_side_effects=True, vmem_limit_bytes=67043328
         ),
     )(
-        laid,
-        short_filter[:, :, None, :],
-        rate_t[:, None, :],
-        coef[:, None, :],
+        projected.transpose(1, 0, 2),
+        short_filter,
+        rate_t,
+        residues.T,
         skip_gain[None, :],
-        rate_t.reshape(modes * groups, 1, 128),
         out_weight.T,
     )
     return out.reshape(steps, SUBS, chans).transpose(1, 0, 2).reshape(rows, chans)

time: 94.2 us -> 77.4 us (0.82)
  local copies, waits for them, and re-layouts: 11.5 us -> 1.73 us
  starting transfers between devices: 4.36 us -> 0 us
  other arithmetic: 2.77 us -> 0 us
    another operation x9 -> x0, local copies, waits for them, and re-layouts: 7 us -> none  [per_device(): jnp.stack([padded[k * steps:k * steps + steps + 2] for k in range(SUBS)],...]
    ppermute x1 -> x0, starting transfers between devices: 4.36 us -> none  [per_device(): lax.ppermute(projected[-2:], 'ctx', [(i, i + 1) for i in range(n_ctx - 1)])]
    another operation x1 -> x0, other arithmetic: 1.75 us -> none  [per_device(): jnp.stack([padded[k * steps:k * steps + steps + 2] for k in range(SUBS)],...]
    broadcast_in_dim x3 -> x0, local copies, waits for them, and re-layouts: 1.56 us -> none  [the longest x1 0.78 us: per_device(): rate_t[:, None, :]]
    transpose x1, local copies, waits for them, and re-layouts: 0.78 us -> 1.73 us  [per_device(): out.reshape(steps, SUBS, chans).transpose(1, 0, 2).reshape(rows, chans)]
  transfers between devices with their start and end apart: 1 -> 0, of which waited for: 0 -> 0; matrix products, arithmetic and copies ran while one was open for 3% -> 0% of each run, Pallas kernels for 0% -> 0%
where the time goes in v2:
time: 77.4 us; the launch traced here: 77.2 us
  Pallas kernels  75.5 us (98%)
  local copies, waits for them, and re-layouts  1.73 us (2%)
    pallas_call x1, Pallas kernels, per_device(): pl.pallas_call(functools.partial(kernel, dims, FIRST, SECOND, SPLIT), out...  75.5 us
    transpose x1, local copies, waits for them, and re-layouts, per_device(): out.reshape(steps, SUBS, chans).transpose(1, 0, 2).reshape(rows, chans)  1.73 us

profile of v2, /device:TPU:1, one launch (start us, length us, event | category | flops | bytes accessed | tf_op | source)
XLA Modules:
  0.0 77.2 jit_solution(3767355515763566951)
XLA Ops:
  0.0 75.5 %shard_map.64 = bf16[256,512]{1,0:T(8,128)(2,1)} custom-call(bf16[3,256,512]{2,1,0:T(8,128)(2,1)} %bitcast.10, f32[3,3,512]{2,1,0:T(4,128)} %taps_in.1, f32[16,512]{1,0:T(8,128)} %bitcast.12, f32[16,512]{1,0:T(8,128)} %bitcast.13, f32[1,512]{1,0:T(1,128)} %bitcast.14, bf16[64,512]{1,0:T(8,128)(2,1)} %bitcast.11), custom_call_target="tpu_custom_call" | custom-call | tf_op jit(solution)/shard_map/pallas_call | solution.py:431
  75.5 1.7 %copy.7 = bf16[8,32,512]{2,1,0:T(8,128)(2,1)} copy(bf16[8,32,512]{2,0,1:T(8,128)(2,1)} %bitcast.9) | data formatting | bytes 524288 | tf_op jit(solution)/shard_map/transpose | solution.py:498

commit v3 on v2

--- a/solution.py
+++ b/solution.py
@@ -11,7 +11,7 @@
 F32 = jnp.float32
 BF16 = jnp.bfloat16
 SUBS = 8
-FIRST, SECOND, SPLIT = 5, 9, 16
+FIRST, SECOND, SPLIT = 6, 9, 16
 
 
 def kernel(
@@ -209,51 +209,59 @@
 
     sub = lax.broadcasted_iota(jnp.int32, (SUBS, 128), 0)
 
+    def lanes_of(q):
+        return pl.ds(q * 128 if isinstance(q, int) else pl.multiple_of(q * 128, 128), 128)
+
     def mixer(q):
-        lanes = pl.ds(q * 128, 128)
+        lanes = lanes_of(q)
         taps = [
             [jnp.broadcast_to(taps_ref[i, pl.ds(s, 1), lanes], (SUBS, 128)) for i in range(3)]
             for s in range(3)
         ]
 
-        def mixed(s, j):
-            return sum(
-                taps[s][i] * pf[s, q, pl.ds(8 + j - i, SUBS, stride=steps), :] for i in range(3)
-            )
-
-        def at_step(j):
-            value = mixed(1, j) * mixed(2, j)
+        def load(j):
+            return tuple(pf[s, q, pl.ds(8 + j, SUBS, stride=steps), :] for s in range(3))
+
+        def at_step(j, now, last, older):
+            mixed = [
+                taps[s][0] * now[s] + taps[s][1] * last[s] + taps[s][2] * older[s]
+                for s in range(3)
+            ]
+            value = mixed[1] * mixed[2]
             gated[j, :, lanes] = value
-            query[j, :, lanes] = mixed(0, j)
+            query[j, :, lanes] = mixed[0]
             return value
 
-        return at_step
+        return load, at_step
 
     def first_pass(q):
         lanes = pl.ds(q * 128, 128)
         decay = [jnp.exp(-row(rate_ref, r, lanes)) for r in range(modes)]
-        at_step = mixer(q)
-
-        def body(j, state):
-            value = at_step(j)
-            return tuple(decay[r] * state[r] + value for r in range(modes))
+        load, at_step = mixer(q)
+
+        def body(j, held):
+            state, last, older = held
+            now = load(j)
+            value = at_step(j, now, last, older)
+            return tuple(decay[r] * state[r] + value for r in range(modes)), now, last
 
         zero = jnp.zeros((SUBS, 128), F32)
-        state = lax.fori_loop(2, steps, body, (zero,) * modes, unroll=2)
+        state, _, _ = lax.fori_loop(2, steps, body, ((zero,) * modes, load(1), load(0)), unroll=2)
         for r in range(modes):
             carry[r, :, lanes] = state[r]
             grow[r, :, lanes] = jnp.exp(
                 -float(steps) * sub.astype(F32) * row(rate_ref, r, lanes)
             )
 
-    def first_steps(q):
-        lanes = pl.ds(q * 128, 128)
+    def first_steps(q, _):
+        lanes = lanes_of(q)
         for s in range(3):
             edge = tail[s, :, lanes].astype(F32)
             pf[s, q, pl.ds(0, 8), :] = jnp.where(me > 0, edge, 0.0)
-        at_step = mixer(q)
-        zeroth = at_step(0)
-        first = at_step(1)
+        load, at_step = mixer(q)
+        before = [load(j) for j in (-2, -1, 0, 1)]
+        zeroth = at_step(0, before[2], before[1], before[0])
+        first = at_step(1, before[3], before[2], before[1])
         for r in range(modes):
             rate = row(rate_ref, r, lanes)
             total = (
@@ -267,6 +275,53 @@
             ends[r * groups + q] = total[SUBS - 1:, :]
             leaps[r * groups + q] = jnp.exp(-float(rows) * rate[:1])
             carry[r, :, lanes] = jnp.where(sub >= 1, pltpu.roll(total, 1, 0), 0.0)
+        return 0
+
+    def depart():
+        pl.semaphore_wait(sem_r4, 2)
+        go_ends()
+        got_ends[me] = ends[me]
+
+    def prefix():
+        wait_ends()
+        leap = leaps[me]
+
+        def body(p, state):
+            inits[p] = state
+            return leap * state + got_ends[p]
+
+        lax.fori_loop(0, n_ctx, body, jnp.zeros((1, 128), F32), unroll=4)
+        go_inits()
+        got_inits[me] = inits[me]
+
+    def finish_conv():
+        wait_inits()
+        def one_group(q, _):
+            lanes = lanes_of(q)
+            decay = [jnp.exp(-row(rate_ref, r, lanes)) for r in range(modes)]
+            coef = [row(coef_ref, r, lanes) for r in range(modes)]
+            skip = row(skip_ref, 0, lanes)
+
+            def second_pass(j, state):
+                value = gated[j, :, lanes]
+                after = tuple(decay[r] * state[r] + value for r in range(modes))
+                terms = [coef[r] * after[r] for r in range(modes)] + [skip * value]
+                while len(terms) > 1:
+                    rest = terms[len(terms) // 2 * 2:]
+                    terms = [a + b for a, b in zip(terms[::2], terms[1::2])] + rest
+                hid[j, :, lanes] = query[j, :, lanes] * terms[0]
+                return after
+
+            begin = tuple(
+                carry[r, :, lanes]
+                + grow[r, :, lanes] * jnp.broadcast_to(got_inits[r * groups + q], (SUBS, 128))
+                for r in range(modes)
+            )
+            lax.fori_loop(0, steps, second_pass, begin, unroll=2)
+            return 0
+
+        lax.fori_loop(0, groups, one_group, 0)
+        hidb[...] = hid[...].reshape(steps * SUBS, chans).astype(BF16)
 
     herald(sem_r1, 1)
     first_pass(0)
@@ -277,70 +332,27 @@
         (lax.rem(me + 1, n_ctx), tp),
     )
     start(send_tail)
+    ring_step(1)
     first_pass(1)
     pl.semaphore_wait(sem_r2, 2)
     herald(sem_r3, 4)
-    for q in range(2, groups):
-        first_pass(q)
+    first_pass(2)
+    ring_step(2)
+    first_pass(3)
     send_tail.wait_recv()
-    for q in range(groups):
-        first_steps(q)
+    lax.fori_loop(0, groups, first_steps, 0)
     pl.semaphore_wait(sem_r3, 2)
     herald(sem_r4, 1)
-
-    def depart():
-        pl.semaphore_wait(sem_r4, 2)
-        go_ends()
-        got_ends[me] = ends[me]
-
-    def prefix():
-        wait_ends()
-        leap = leaps[me]
-
-        def body(p, state):
-            inits[p] = state
-            return leap * state + got_ends[p]
-
-        lax.fori_loop(0, n_ctx, body, jnp.zeros((1, 128), F32), unroll=4)
-        go_inits()
-        got_inits[me] = inits[me]
-
-    def finish_conv():
-        wait_inits()
-        for q in range(groups):
-            lanes = pl.ds(q * 128, 128)
-
-            decay = [jnp.exp(-row(rate_ref, r, lanes)) for r in range(modes)]
-            coef = [row(coef_ref, r, lanes) for r in range(modes)]
-            skip = row(skip_ref, 0, lanes)
-
-            def second_pass(j, state):
-                value = gated[j, :, lanes]
-                after = tuple(decay[r] * state[r] + value for r in range(modes))
-                terms = [coef[r] * after[r] for r in range(modes)] + [skip * value]
-                while len(terms) > 1:
-                    rest = terms[len(terms) // 2 * 2:]
-                    terms = [a + b for a, b in zip(terms[::2], terms[1::2])] + rest
-                hid[j, :, lanes] = query[j, :, lanes] * terms[0]
-                return after
-
-            begin = tuple(
-                carry[r, :, lanes]
-                + grow[r, :, lanes] * jnp.broadcast_to(got_inits[r * groups + q], (SUBS, 128))
-                for r in range(modes)
-            )
-            lax.fori_loop(0, steps, second_pass, begin, unroll=2)
-        hidb[...] = hid[...].reshape(steps * SUBS, chans).astype(BF16)
-
-    for s in range(1, ring + 2):
-        if s == 2:
-            depart()
+    ring_step(3)
+    depart()
+    for s in range(4, ring + 1):
         if s == first_wait:
             prefix()
         if s == second_wait:
             finish_conv()
-        if s <= ring:
-            ring_step(s)
+        ring_step(s)
+    if second_wait > ring:
+        finish_conv()
     relay_bx(-ring)
     for e in range(nz):
         w_copy(hi, x + 2, z + e, sem_xbr, (e,), x_up).wait_recv()
@@ -354,16 +366,21 @@
             hidb[...], block, (((1,), (1,)), ((), ())), preferred_element_type=F32
         )
 
-    order = [2, 1, ny - 1, 0]
-
     def pair_copy(i):
         return remote(to_pair.at[i], from_pair.at[i], sem_pair.at[0, i], sem_pair.at[1, i], pair)
 
-    for i, dy in enumerate(order):
-        to_pair[i] = project(lax.rem(y + dy, ny), 1 - core).astype(BF16)
-        start(pair_copy(i))
-    for i, dy in enumerate(order):
-        own[i] = project(lax.rem(y + dy, ny), core)
+    def for_pair(i, _):
+        to_pair[i] = project(lax.rem(y + 2 - i + ny, ny), 1 - core).astype(BF16)
+        pair_copy(i).start()
+        return 0
+
+    def for_own(i, _):
+        own[i] = project(lax.rem(y + 2 - i + ny, ny), core)
+        return 0
+
+    lax.fori_loop(0, ny, for_pair, 0)
+    lax.fori_loop(0, ny, for_own, 0)
+    pending.extend(pair_copy(i) for i in range(ny))
 
     def top(ref):
         return ref.at[pl.ds(0, half)]
@@ -389,8 +406,8 @@
     pair_copy(1).wait_recv()
     fin_up[lo_rows] = (own[1, lo_rows] + from_pair[1, lo_rows].astype(F32)).astype(BF16)
     start(up_bottom)
-    pair_copy(2).wait_recv()
-    fin_dn[hi_rows] = (own[2, hi_rows] + from_pair[2, hi_rows].astype(F32)).astype(BF16)
+    pair_copy(3).wait_recv()
+    fin_dn[hi_rows] = (own[3, hi_rows] + from_pair[3, hi_rows].astype(F32)).astype(BF16)
     start(dn_top)
     far_up.wait_recv()
     fin_up[hi_rows] = (
@@ -399,16 +416,16 @@
     start(up_top)
     far_dn.wait_recv()
     fin_dn[lo_rows] = (
-        own[2, lo_rows] + from_pair[2, lo_rows].astype(F32) + relay_dn[...].astype(F32)
+        own[3, lo_rows] + from_pair[3, lo_rows].astype(F32) + relay_dn[...].astype(F32)
     ).astype(BF16)
     start(dn_bottom)
-    pair_copy(3).wait_recv()
-    own[3] = own[3] + from_pair[3].astype(F32)
+    pair_copy(2).wait_recv()
+    own[2] = own[2] + from_pair[2].astype(F32)
     up_bottom.wait_recv()
     dn_top.wait_recv()
     up_top.wait_recv()
     dn_bottom.wait_recv()
-    out_ref[...] = (own[3] + got_up[...].astype(F32) + got_dn[...].astype(F32)).astype(BF16)
+    out_ref[...] = (own[2] + got_up[...].astype(F32) + got_dn[...].astype(F32)).astype(BF16)
 
     sent_ends()
     sent_inits()

time: 77.4 us -> 73.8 us (0.953)
  Pallas kernels: 75.5 us -> 71.9 us
    pallas_call x1, Pallas kernels: 75.5 us -> 71.9 us  [per_device(): pl.pallas_call(functools.partial(kernel, dims, FIRST, SECOND, SPLIT), out...]
where the time goes in v3:
time: 73.8 us; the launch traced here: 73.6 us
  Pallas kernels  71.9 us (97%)
  local copies, waits for them, and re-layouts  1.73 us (2%)
    pallas_call x1, Pallas kernels, per_device(): pl.pallas_call(functools.partial(kernel, dims, FIRST, SECOND, SPLIT), out...  71.9 us
    transpose x1, local copies, waits for them, and re-layouts, per_device(): out.reshape(steps, SUBS, chans).transpose(1, 0, 2).reshape(rows, chans)  1.73 us

profile of v3, /device:TPU:1, one launch (start us, length us, event | category | flops | bytes accessed | tf_op | source)
XLA Modules:
  0.0 73.6 jit_solution(16027740393615223820)
XLA Ops:
  0.0 71.9 %shard_map.64 = bf16[256,512]{1,0:T(8,128)(2,1)} custom-call(bf16[3,256,512]{2,1,0:T(8,128)(2,1)} %bitcast.10, f32[3,3,512]{2,1,0:T(4,128)} %taps_in.1, f32[16,512]{1,0:T(8,128)} %bitcast.12, f32[16,512]{1,0:T(8,128)} %bitcast.13, f32[1,512]{1,0:T(1,128)} %bitcast.14, bf16[64,512]{1,0:T(8,128)(2,1)} %bitcast.11), custom_call_target="tpu_custom_call" | custom-call | tf_op jit(solution)/shard_map/pallas_call | solution.py:448
  71.9 1.7 %copy.7 = bf16[8,32,512]{2,1,0:T(8,128)(2,1)} copy(bf16[8,32,512]{2,0,1:T(8,128)(2,1)} %bitcast.9) | data formatting | bytes 524288 | tf_op jit(solution)/shard_map/transpose | solution.py:515

commit v4 on v3

--- a/solution.py
+++ b/solution.py
@@ -69,18 +69,7 @@
         pl.semaphore_signal(barrier, inc=1, device_id=other, device_id_type=MESH)
 
     rows = steps * SUBS
-    for load in loads:
-        load.wait()
-    twice = 2.0 * rate_ref[...]
-    small = jnp.ones_like(twice)
-    for k in range(9, 1, -1):
-        small = 1.0 - small * twice * (1.0 / k)
-    lost = jnp.where(twice < 0.25, twice * small, 1.0 - jnp.exp(-twice))
-    coef_ref[...] = res_ref[...] * jnp.sqrt(lost)
-    for s in range(3):
-        for q in range(groups):
-            pf[s, q, pl.ds(8, rows), :] = p_ref[s, :, pl.ds(q * 128, 128)].astype(F32)
-
+    loads[0].wait()
     pl.semaphore_wait(barrier, len(near))
 
     pending = []
@@ -190,9 +179,10 @@
                 w_copy(lo, x + dx, z + s, sem_zam, (s, dx), z_dn).wait_recv()
                 if s < ring - 1:
                     send_am(s + 1, dx)
-        relay_bx(-(s - 1))
         if s > 1:
-            relay_bx(s - 1)
+            relay_bx(-(s - 2))
+        if s > 2:
+            relay_bx(s - 2)
 
     go_ends, wait_ends, sent_ends = exchange(ends, got_ends, sem_e)
     go_inits, wait_inits, sent_inits = exchange(inits, got_inits, sem_i)
@@ -324,6 +314,18 @@
         hidb[...] = hid[...].reshape(steps * SUBS, chans).astype(BF16)
 
     herald(sem_r1, 1)
+    for load in loads[1:]:
+        load.wait()
+    twice = 2.0 * rate_ref[...]
+    small = jnp.ones_like(twice)
+    for k in range(9, 1, -1):
+        small = 1.0 - small * twice * (1.0 / k)
+    lost = jnp.where(twice < 0.25, twice * small, 1.0 - jnp.exp(-twice))
+    coef_ref[...] = res_ref[...] * jnp.sqrt(lost)
+    for s in range(3):
+        for q in range(groups):
+            pf[s, q, pl.ds(8, rows), :] = p_ref[s, :, pl.ds(q * 128, 128)].astype(F32)
+
     first_pass(0)
     pl.semaphore_wait(sem_r1, 2)
     herald(sem_r2, 2)
@@ -353,6 +355,8 @@
         ring_step(s)
     if second_wait > ring:
         finish_conv()
+    relay_bx(1 - ring)
+    relay_bx(ring - 1)
     relay_bx(-ring)
     for e in range(nz):
         w_copy(hi, x + 2, z + e, sem_xbr, (e,), x_up).wait_recv()

time: 73.8 us -> 74.1 us (level)
  no operation moved by 1% of the time
where the time goes in v4:
time: 74.1 us; the launch traced here: 73.9 us
  Pallas kernels  72.2 us (97%)
  local copies, waits for them, and re-layouts  1.73 us (2%)
    pallas_call x1, Pallas kernels, per_device(): pl.pallas_call(functools.partial(kernel, dims, FIRST, SECOND, SPLIT), out...  72.2 us
    transpose x1, local copies, waits for them, and re-layouts, per_device(): out.reshape(steps, SUBS, chans).transpose(1, 0, 2).reshape(rows, chans)  1.73 us

profile of v4, /device:TPU:1, one launch (start us, length us, event | category | flops | bytes accessed | tf_op | source)
XLA Modules:
  0.0 73.9 jit_solution(1531386378477914474)
XLA Ops:
  0.0 72.2 %shard_map.64 = bf16[256,512]{1,0:T(8,128)(2,1)} custom-call(bf16[3,256,512]{2,1,0:T(8,128)(2,1)} %bitcast.10, f32[3,3,512]{2,1,0:T(4,128)} %taps_in.1, f32[16,512]{1,0:T(8,128)} %bitcast.12, f32[16,512]{1,0:T(8,128)} %bitcast.13, f32[1,512]{1,0:T(1,128)} %bitcast.14, bf16[64,512]{1,0:T(8,128)(2,1)} %bitcast.11), custom_call_target="tpu_custom_call" | custom-call | tf_op jit(solution)/shard_map/pallas_call | solution.py:452
  72.2 1.7 %copy.7 = bf16[8,32,512]{2,1,0:T(8,128)(2,1)} copy(bf16[8,32,512]{2,0,1:T(8,128)(2,1)} %bitcast.9) | data formatting | bytes 524288 | tf_op jit(solution)/shard_map/transpose | solution.py:519
